TPU v7x, 32 devices: a whole 2x2x4 slice. The times are simulated.
32 devices in a mesh: dp: 8 (over z, x), tensor: 4 (over y, core).
Axes of the slice: x: 2, y: 2, z: 4, core: 2. Of those that a mesh axis runs over, the one named last changes fastest.
Arguments:
- inputs: bfloat16 [8192, 4096], P('dp'), may hold values from -6 to 6
- out_grads: bfloat16 [8192, 6144], P('dp', 'tensor'), may hold values from -0.01953125 to 0.01953125
- left_factor: float32 [4096, 4096], P('dp', 'tensor'), may hold values from -6 to 6
- right_factor: float32 [6144, 6144], P('dp', 'tensor'), may hold values from -6 to 6
- left_basis: float32 [4096, 4096], P('dp', 'tensor'), may hold values from -0.09375 to 0.09375
- right_basis: float32 [6144, 6144], P('dp', 'tensor'), may hold values from -0.078125 to 0.078125
Outputs:
- left_new: float32 [4096, 4096], P('dp', 'tensor')
- right_new: float32 [6144, 6144], P('dp', 'tensor')
- rotated: float32 [4096, 6144], P('dp', 'tensor')
All inputs are finite; a program needn't handle non-finite values.
Results may differ from a plain program's by a relative error of at most 0.019.
Values may be sent and summed in bfloat16 or wider, within the bound.
A program may use at most 192 MiB of HBM per device.

v0:
```python
import jax
import jax.numpy as jnp
from jax import lax
from jax.sharding import PartitionSpec as P

F32 = jnp.float32
BF16 = jnp.bfloat16


def mm(a, b, ca, cb):
    return lax.dot_general(a, b, (((ca,), (cb,)), ((), ())), preferred_element_type=F32)


def spread(block, owner, n_dp, n_t):
    me = lax.axis_index("tensor")
    mine = lax.rem(me - owner(lax.axis_index("dp")) + n_t, n_t)
    step = 1
    while step < n_t:
        pairs = []
        for d in range(n_dp):
            for k in range(step):
                if k + step < n_t:
                    src = (owner(d) + k) % n_t
                    dst = (owner(d) + k + step) % n_t
                    pairs.append((d * n_t + src, d * n_t + dst))
        got = lax.ppermute(block, ("dp", "tensor"), pairs)
        block = jnp.where((mine >= step) & (mine < 2 * step), got, block)
        step *= 2
    return block


def shards(inputs, out_grads, left_factor, right_factor, left_basis, right_basis):
    n_dp, n_t = (lax.axis_size("dp"), lax.axis_size("tensor"))
    krows, kcols = left_factor.shape
    mrows, mcols = right_factor.shape
    dp = lax.axis_index("dp")
    left_low = left_basis.astype(BF16)
    left_rows = lax.all_gather(left_low, "tensor", axis=1, tiled=True)
    left_cols = lax.all_to_all(left_rows, "dp", split_axis=1, concat_axis=0, tiled=True)
    basis_panel = lax.all_gather(right_basis.astype(BF16), "dp", axis=0, tiled=True)
    summed = lax.psum_scatter(
        mm(inputs, out_grads, 0, 0).astype(BF16), "dp", scatter_dimension=0, tiled=True
    )
    col_panel = lax.all_gather(summed, "dp", axis=0, tiled=True)
    turned = mm(left_cols, col_panel, 0, 0).astype(BF16)
    turned_rows = lax.all_gather(turned, "tensor", axis=1, tiled=True)
    own = lax.dynamic_slice_in_dim(col_panel, lax.rem(dp * mrows, mcols), mrows, 1)
    own = spread(own, lambda d: d * mrows // mcols, n_dp, n_t)
    parts = jnp.einsum(
        "jkc,rc->jrk", col_panel.reshape(n_t, kcols, mcols), summed, preferred_element_type=F32
    ).astype(BF16)
    gram_left = lax.psum_scatter(
        parts.reshape(n_t * krows, kcols), "tensor", scatter_dimension=0, tiled=True
    ).astype(F32)
    left_new = 0.95 * left_factor + 0.05 * gram_left
    right_new = 0.95 * right_factor + 0.05 * mm(own, col_panel, 0, 0)
    rotated = mm(turned_rows, basis_panel, 1, 0)
    return (left_new, right_new, rotated)


def solution(mesh):
    spec = P("dp", "tensor")
    return jax.shard_map(
        shards,
        mesh=mesh,
        in_specs=(P("dp", None), spec, spec, spec, spec, spec),
        out_specs=(spec, spec, spec),
        check_vma=False,
    )
```

profile of v0, /device:TPU:0, one launch (start us, length us, event | category | flops | bytes accessed | tf_op | source)
XLA Modules:
  0.0 975.2 jit_solution(8591873962908227927)
XLA Ops:
  7.2 0.0 reduce-scatter.3.cloned.1.call-start
  7.2 1.8 copy-done
  9.1 19.1 %convolution_convert_fusion = bf16[4096,1536]{1,0:T(8,128)(2,1)} fusion(bf16[1024,4096]{1,0:T(8,128)(2,1)} %param.6, bf16[1024,1536]{1,0:T(8,128)(2,1)S(1)} %copy-done), kind=kOutput, calls=%fused_computation | convolution fusion | flops 12891193344 | bytes 24117248 | tf_op jit(solution)/shard_map/dot_general | solution.py:11
  28.2 0.0 reduce-scatter.3.cloned.1.call-update
  28.2 0.0 all-gather.5.cloned.1.call-start
  28.3 210.1 %reduce-scatter.3.cloned.1.call-done = bf16[512,1536]{1,0:T(8,128)(2,1)} async-done(((bf16[4096,1536]{1,0:T(8,128)(2,1)}), bf16[512,1536]{1,0:T(8,128)(2,1)}) %reduce-scatter.3.cloned.1.call-update) | async-done | bytes 1572880 | tf_op jit(solution)/shard_map/reduce_scatter | solution.py:41
  238.4 0.0 all-gather.7.cloned.1.call-start
  238.4 1.4 copy.9
  239.8 0.0 all-gather.7.cloned.1.call-update
  239.8 0.0 reduce-scatter.5.cloned.1.call-start
  239.9 176.2 %all-gather.5.cloned.1.call-done = bf16[4096,1536]{1,0:T(8,128)(2,1)} async-done(((bf16[512,1536]{1,0:T(8,128)(2,1)}), bf16[4096,1536]{1,0:T(8,128)(2,1)}) %all-gather.5.cloned.1.call-update) | async-done | bytes 12582928 | tf_op jit(solution)/shard_map/all_gather | solution.py:44
  416.1 11.4 %convolution_convert_fusion.2 = bf16[512,4,1024]{2,0,1:T(8,128)(2,1)} fusion(bf16[4,1024,1536]{2,1,0:T(8,128)(2,1)} %bitcast.20, bf16[512,1536]{1,0:T(8,128)(2,1)} %reduce-scatter.3.cloned.1.call-done), kind=kOutput, calls=%fused_computation.8 | convolution fusion | flops 6444548096 | bytes 18350080 | tf_op jit(solution)/shard_map/jkc,rc->jrk/dot_general | solution.py:49
  427.5 0.0 reduce-scatter.5.cloned.1.call-update
  427.6 0.0 all-gather.11.cloned.1.call-start
  427.6 4.0 convert_element_type.31
  431.6 0.0 all-gather.11.cloned.1.call-update
  431.7 19.3 %all-gather.7.cloned.1.call-done = bf16[512,4096]{0,1:T(8,128)(2,1)} async-done(((bf16[512,1024]{0,1:T(8,128)(2,1)}), bf16[512,4096]{0,1:T(8,128)(2,1)}) %all-gather.7.cloned.1.call-update) | async-done | bytes 4194320 | tf_op jit(solution)/shard_map/all_gather | solution.py:38
  450.9 5.5 all-to-all-start
  456.4 0.0 all-gather.9.cloned.1.call-start
  456.5 9.8 %constant_dynamic-slice_fusion = bf16[4096,768]{1,0:T(8,128)(2,1)} fusion(bf16[4096,1536]{1,0:T(8,128)(2,1)} %all-gather.5.cloned.1.call-done, s32[]{:T(128)S(6)} %select_n.25), kind=kLoop, calls=%fused_computation.11 | loop fusion | bytes 12582916 | tf_op jit(solution)/shard_map/dynamic_slice | solution.py:47
  466.3 4.3 collective-permute-start
  470.6 101.8 %all-to-all-done = bf16[512,8,512]{0,2,1:T(8,128)(2,1)} async-done(((bf16[512,8,512]{0,2,1:T(8,128)(2,1)}), bf16[512,8,512]{0,2,1:T(8,128)(2,1)}, u32[]{:S(2)}, u32[]{:S(2)}) %all-to-all-start) | async-done | bytes 4194336 | tf_op jit(solution)/shard_map/all_to_all | solution.py:39
  572.4 6.5 copy.10
  578.9 11.9 %fusion.5 = bf16[512,1536]{0,1:T(8,128)(2,1)} fusion(bf16[4096,1536]{1,0:T(8,128)(2,1)} %all-gather.5.cloned.1.call-done, bf16[4096,512]{1,0:T(8,128)(2,1)} %bitcast.23), kind=kOutput, calls=%fused_computation.7 | convolution fusion | flops 6443237376 | bytes 18350080 | tf_op jit(solution)/shard_map/dot_general | solution.py:11
  590.8 0.0 all-gather.9.cloned.1.call-update
  590.9 10.3 %broadcast_select_fusion = bf16[4096,768]{1,0:T(8,128)(2,1)} fusion(bf16[4096,768]{1,0:T(8,128)(2,1)} %collective-permute-done, pred[]{:T(512)S(6)} %and.15, bf16[4096,1536]{1,0:T(8,128)(2,1)} %all-gather.5.cloned.1.call-done, s32[]{:T(128)S(6)} %select_n.25), kind=kLoop, calls=%fused_computation.3 | loop fusion | flops 3145728 | bytes 18874372 | tf_op jit(solution)/shard_map/jit(_where)/select_n | solution.py:27
  601.1 5.2 collective-permute-start.1
  606.4 3.0 multiply_add_fusion.1
  609.4 274.1 %all-gather.11.cloned.1.call-done = bf16[6144,1536]{1,0:T(8,128)(2,1)} async-done(((bf16[768,1536]{1,0:T(8,128)(2,1)}), bf16[6144,1536]{1,0:T(8,128)(2,1)}) %all-gather.11.cloned.1.call-update) | async-done | bytes 18874384 | tf_op jit(solution)/shard_map/all_gather | solution.py:40
  883.6 49.6 %all-gather.9.cloned.1.call-done = bf16[512,6144]{0,1:T(8,128)(2,1)} async-done(((bf16[512,1536]{0,1:T(8,128)(2,1)}), bf16[512,6144]{0,1:T(8,128)(2,1)}) %all-gather.9.cloned.1.call-update) | async-done | bytes 6291472 | tf_op jit(solution)/shard_map/all_gather | solution.py:46
  933.2 16.9 %fusion.7 = f32[512,1536]{1,0:T(8,128)} fusion(bf16[512,6144]{0,1:T(8,128)(2,1)} %all-gather.9.cloned.1.call-done, bf16[6144,1536]{1,0:T(8,128)(2,1)} %all-gather.11.cloned.1.call-done), kind=kOutput, calls=%fused_computation.12 | convolution fusion | flops 9663676416 | bytes 28311552 | tf_op jit(solution)/shard_map/dot_general | solution.py:11
  950.1 18.2 %multiply_add_fusion = f32[768,1536]{1,0:T(8,128)} fusion(f32[768,1536]{1,0:T(8,128)} %param.9, bf16[4096,1536]{1,0:T(8,128)(2,1)} %all-gather.5.cloned.1.call-done, bf16[4096,768]{1,0:T(8,128)(2,1)} %collective-permute-done.1, bf16[4096,768]{1,0:T(8,128)(2,1)} %broadcast_select_fusion, pred[]{:T(512)S(6)} %and.14), kind=kOutput, calls=%fused_computation.5 | convolution fusion | flops 9670361088 | bytes 34603008 | tf_op jit(solution)/shard_map/dot_general | solution.py:11
  (11 shorter events, 0.0 us)
Async XLA Ops:
  7.2 1.9 copy-start
  7.2 231.2 %reduce-scatter.3.cloned.1.call-start = ((), (), s32[]{:S(2)}) async-start(), calls=%async_computation.3 | async-start | bytes 14155776 | tf_op jit(solution)/shard_map/reduce_scatter | solution.py:41
  28.2 210.2 %copy-start.2 = (f32[512,1024]{1,0:T(8,128)S(1)}, f32[512,1024]{1,0:T(8,128)}, u32[]{:S(2)}) copy-start(f32[512,1024]{1,0:T(8,128)} %param.10) | copy-start | bytes 6291460
  28.2 387.9 %all-gather.5.cloned.1.call-start = ((), (), s32[]{:S(2)}) async-start(), calls=%async_computation.4 | async-start | bytes 14155776 | tf_op jit(solution)/shard_map/all_gather | solution.py:44
  238.4 212.6 %all-gather.7.cloned.1.call-start = ((), (), s32[]{:S(2)}) async-start(), calls=%async_computation.6 | async-start | bytes 5242880 | tf_op jit(solution)/shard_map/all_gather | solution.py:38
  239.8 366.6 %reduce-scatter.5.cloned.1.call-start = ((), (), s32[]{:S(2)}) async-start(), calls=%async_computation.5 | async-start | bytes 5242880 | tf_op jit(solution)/shard_map/reduce_scatter | solution.py:52
  427.6 456.0 %all-gather.11.cloned.1.call-start = ((), (), s32[]{:S(2)}) async-start(), calls=%async_computation.8 | async-start | bytes 21233664 | tf_op jit(solution)/shard_map/all_gather | solution.py:40
  450.9 121.4 %all-to-all-start = ((bf16[512,8,512]{0,2,1:T(8,128)(2,1)}), bf16[512,8,512]{0,2,1:T(8,128)(2,1)}, u32[]{:S(2)}, u32[]{:S(2)}) async-start(bf16[512,8,512]{0,2,1:T(8,128)(2,1)} %bitcast.22), calls=%async_computation.2 | async-start | bytes 8388608 | tf_op jit(solution)/shard_map/all_to_all | solution.py:39
  456.4 476.8 %all-gather.9.cloned.1.call-start = ((), (), s32[]{:S(2)}) async-start(), calls=%async_computation.7 | async-start | bytes 7864320 | tf_op jit(solution)/shard_map/all_gather | solution.py:46
  466.3 124.5 %collective-permute-start = (bf16[4096,768]{1,0:T(8,128)(2,1)}, bf16[4096,768]{1,0:T(8,128)(2,1)}, u32[]{:S(2)}, u32[]{:S(2)}) collective-permute-start(bf16[4096,768]{1,0:T(8,128)(2,1)} %constant_dynamic-slice_fusion), channel_id=1, source_target_pairs={{0,1},{4,5},{9,10},{13,14},{18,19},{22,23},{27,24},{31,28}} | collective-permute-start | bytes 18874376 | tf_op jit(solution)/shard_map/ppermute | solution.py:26
  590.8 15.6 %copy-start.3 = (f32[512,1024]{1,0:T(8,128)S(1)}, f32[512,1024]{1,0:T(8,128)}, u32[]{:S(2)}) copy-start(f32[512,1024]{1,0:T(8,128)} %param.8) | copy-start | bytes 6291460
  601.1 349.0 %collective-permute-start.1 = (bf16[4096,768]{1,0:T(8,128)(2,1)}, bf16[4096,768]{1,0:T(8,128)(2,1)}, u32[]{:S(2)}, u32[]{:S(2)}) collective-permute-start(bf16[4096,768]{1,0:T(8,128)(2,1)} %broadcast_select_fusion), channel_id=1, source_target_pairs={{0,2},{1,3},{4,6},{5,7},{9,11},{10,8},{13,15},{14,12},{18,16},{19,... | collective-permute-start | bytes 18874376 | tf_op jit(solution)/shard_map/ppermute | solution.py:26
  950.1 18.2 %copy-start.1 = (bf16[1024,1536]{1,0:T(8,128)(2,1)S(1)}, bf16[1024,1536]{1,0:T(8,128)(2,1)}, u32[]{:S(2)}) copy-start(bf16[1024,1536]{1,0:T(8,128)(2,1)} %param.7) | copy-start | bytes 9437188
Sparse Core Ops, SparseCore 0:
  28.4 209.9 reduce-scatter.2
  240.6 175.4 all-gather.4
  418.2 32.6 all-gather.6
  453.9 44.5 reduce-scatter.4
  500.5 383.0 all-gather.10
  885.1 48.1 all-gather.8
where the time goes:
time: 976 us; the launch traced here: 975 us
  waiting for transfers between devices  831 us (85%)
  matrix products  77.6 us (8%)
  local copies, waits for them, and re-layouts  19.6 us (2%)
  other arithmetic  17.4 us (2%)
  starting transfers between devices  15.3 us (2%)
  between operations  14.2 us (1%)
    all_gather x1, waiting for transfers between devices, shards(): lax.all_gather(right_basis.astype(BF16), 'dp', axis=0, tiled=True)  274 us
    reduce_scatter x1, waiting for transfers between devices, shards(): lax.psum_scatter(mm(inputs, out_grads, 0, 0).astype(BF16), 'dp', scatter_...  210 us
    all_gather x1, waiting for transfers between devices, shards(): col_panel = lax.all_gather(summed, 'dp', axis=0, tiled=True)  176 us
    all_to_all x1, waiting for transfers between devices, shards(): lax.all_to_all(left_rows, 'dp', split_axis=1, concat_axis=0, tiled=True)  102 us
    dot_general x4, matrix products, mm(): lax.dot_general(a, b, (((ca,), (cb,)), ((), ())), preferred_element_type=...  66.1 us
    all_gather x1, waiting for transfers between devices, shards(): turned_rows = lax.all_gather(turned, 'tensor', axis=1, tiled=True)  49.6 us
  transfers between devices with their start and end apart: 9, of which 6 were waited for; matrix products, arithmetic and copies ran while one was open for 8% of the time, Pallas kernels for 0%

commit v1 on v0

--- a/solution.py
+++ b/solution.py
@@ -37,7 +37,23 @@
     left_low = left_basis.astype(BF16)
     left_rows = lax.all_gather(left_low, "tensor", axis=1, tiled=True)
     left_cols = lax.all_to_all(left_rows, "dp", split_axis=1, concat_axis=0, tiled=True)
-    basis_panel = lax.all_gather(right_basis.astype(BF16), "dp", axis=0, tiled=True)
+    value = right_basis.astype(BF16)
+    size, index, width = (lax.axis_size("dp"), lax.axis_index("dp"), value.shape[0])
+    ahead = [(i, (i + 1) % size) for i in range(size)]
+    left = [(i, (i - 1) % size) for i in range(size)]
+    out = jnp.zeros((*value.shape[:0], size * width, *value.shape[0 + 1 :]), value.dtype)
+    out = lax.dynamic_update_slice_in_dim(out, value, index * width, axis=0)
+    from_left = from_right = value
+    halfway = size // 2
+    for turn in range(1, halfway + 1):
+        from_left = lax.ppermute(from_left, "dp", ahead)
+        out = lax.dynamic_update_slice_in_dim(out, from_left, (index - turn) % size * width, axis=0)
+        if turn < size - halfway:
+            from_right = lax.ppermute(from_right, "dp", left)
+            out = lax.dynamic_update_slice_in_dim(
+                out, from_right, (index + turn) % size * width, axis=0
+            )
+    basis_panel = out
     summed = lax.psum_scatter(
         mm(inputs, out_grads, 0, 0).astype(BF16), "dp", scatter_dimension=0, tiled=True
     )

time: 976 us -> 945 us (0.968)
  waiting for transfers between devices: 831 us -> 745 us
  local copies, waits for them, and re-layouts: 19.6 us -> 48.9 us
  starting transfers between devices: 15.3 us -> 34.2 us
    ppermute x0 -> x7, waiting for transfers between devices: none -> 291 us  [the longest x4 291 us: shards(): from_left = lax.ppermute(from_left, 'dp', ahead)]
    all_gather x1 -> x0, waiting for transfers between devices: 274 us -> none  [shards(): lax.all_gather(right_basis.astype(BF16), 'dp', axis=0, tiled=True)]
    all_to_all x1, waiting for transfers between devices: 102 us -> 0.01 us  [shards(): lax.all_to_all(left_rows, 'dp', split_axis=1, concat_axis=0, tiled=True)]
    all_gather x1, waiting for transfers between devices: 176 us -> 246 us  [shards(): col_panel = lax.all_gather(summed, 'dp', axis=0, tiled=True)]
    all_gather x1, waiting for transfers between devices: 49.6 us -> 0.01 us  [shards(): turned_rows = lax.all_gather(turned, 'tensor', axis=1, tiled=True)]
    dynamic_update_slice x0 -> x7, local copies, waits for them, and re-layouts: none -> 21.2 us  [the longest x4 11.4 us: shards(): lax.dynamic_update_slice_in_dim(out, from_left, (index - turn) % size * w...]
    all_gather x1, waiting for transfers between devices: 19.3 us -> 0.02 us  [shards(): left_rows = lax.all_gather(left_low, 'tensor', axis=1, tiled=True)]
    ppermute x0 -> x7, starting transfers between devices: none -> 16.4 us  [the longest x4 8.96 us: shards(): from_left = lax.ppermute(from_left, 'dp', ahead)]
  transfers between devices with their start and end apart: 9 -> 15, of which waited for: 6 -> 6; matrix products, arithmetic and copies ran while one was open for 8% -> 11% of each run, Pallas kernels for 0% -> 0%
where the time goes in v1:
time: 945 us; the launch traced here: 944 us
  waiting for transfers between devices  745 us (79%)
  matrix products  84.4 us (9%)
  local copies, waits for them, and re-layouts  48.9 us (5%)
  starting transfers between devices  34.2 us (4%)
  other arithmetic  15.8 us (2%)
  between operations  15.8 us (2%)
    ppermute x4, waiting for transfers between devices, shards(): from_left = lax.ppermute(from_left, 'dp', ahead)  291 us
    all_gather x1, waiting for transfers between devices, shards(): col_panel = lax.all_gather(summed, 'dp', axis=0, tiled=True)  246 us
    reduce_scatter x1, waiting for transfers between devices, shards(): lax.psum_scatter(mm(inputs, out_grads, 0, 0).astype(BF16), 'dp', scatter_...  207 us
    dot_general x4, matrix products, mm(): lax.dot_general(a, b, (((ca,), (cb,)), ((), ())), preferred_element_type=...  66.2 us
  transfers between devices with their start and end apart: 15, of which 6 were waited for; matrix products, arithmetic and copies ran while one was open for 11% of the time, Pallas kernels for 0%

profile of v1, /device:TPU:0, one launch (start us, length us, event | category | flops | bytes accessed | tf_op | source)
XLA Modules:
  0.0 943.6 jit_solution(3420228233270420374)
XLA Ops:
  9.9 19.2 %convolution_convert_fusion = bf16[4096,1536]{1,0:T(8,128)(2,1)} fusion(bf16[1024,4096]{1,0:T(8,128)(2,1)} %param.6, bf16[1024,1536]{1,0:T(8,128)(2,1)S(1)} %copy-done), kind=kOutput, calls=%fused_computation | convolution fusion | flops 12891193344 | bytes 24117248 | tf_op jit(solution)/shard_map/dot_general | solution.py:11
  32.1 207.1 %reduce-scatter.3.cloned.1.call-done = bf16[512,1536]{1,0:T(8,128)(2,1)} async-done(((bf16[4096,1536]{1,0:T(8,128)(2,1)}), bf16[512,1536]{1,0:T(8,128)(2,1)}) %reduce-scatter.3.cloned.1.call-update) | async-done | bytes 1572880 | tf_op jit(solution)/shard_map/reduce_scatter | solution.py:57
  239.3 4.7 all-to-all-start
  244.0 246.0 %all-gather.4.cloned.1.call-done = bf16[4096,1536]{1,0:T(8,128)(2,1)} async-done(((bf16[512,1536]{1,0:T(8,128)(2,1)}), bf16[4096,1536]{1,0:T(8,128)(2,1)}) %all-gather.4.cloned.1.call-update) | async-done | bytes 12582928 | tf_op jit(solution)/shard_map/all_gather | solution.py:60
  490.0 18.3 %convolution_convert_fusion.2 = bf16[512,4,1024]{2,0,1:T(8,128)(2,1)} fusion(bf16[4,1024,1536]{2,1,0:T(8,128)(2,1)} %bitcast.20, bf16[512,1536]{1,0:T(8,128)(2,1)S(1)} %copy-done.4), kind=kOutput, calls=%fused_computation.8 | convolution fusion | flops 6444548096 | bytes 18350080 | tf_op jit(solution)/shard_map/jkc,rc->jrk/dot_general | solution.py:65
  508.4 9.8 %constant_dynamic-slice_fusion = bf16[4096,768]{1,0:T(8,128)(2,1)} fusion(bf16[4096,1536]{1,0:T(8,128)(2,1)} %all-gather.4.cloned.1.call-done, s32[]{:T(128)S(6)} %select_n.79), kind=kLoop, calls=%fused_computation.19 | loop fusion | bytes 12582916 | tf_op jit(solution)/shard_map/dynamic_slice | solution.py:63
  518.2 4.8 collective-permute-start
  523.1 6.7 broadcast_in_dim.3
  529.7 2.6 constant_dynamic-update-slice_fusion.7
  533.8 6.4 copy.10
  540.2 11.8 %fusion.5 = bf16[512,1536]{0,1:T(8,128)(2,1)} fusion(bf16[4096,1536]{1,0:T(8,128)(2,1)} %all-gather.4.cloned.1.call-done, bf16[4096,512]{1,0:T(8,128)(2,1)} %bitcast.25), kind=kOutput, calls=%fused_computation.7 | convolution fusion | flops 6443237376 | bytes 18350080 | tf_op jit(solution)/shard_map/dot_general | solution.py:11
  552.1 3.2 collective-permute-start.3
  555.3 78.3 %collective-permute-done.2 = bf16[768,1536]{1,0:T(8,128)(2,1)S(1)} collective-permute-done((bf16[768,1536]{1,0:T(8,128)(2,1)}, bf16[768,1536]{1,0:T(8,128)(2,1)S(1)}, u32[]{:S(2)}, u32[]{:S(2)}) %collective-permute-start.2) | collective-permute-done | bytes 2359328 | tf_op jit(solution)/shard_map/ppermute | solution.py:49
  633.6 2.4 collective-permute-start.4
  636.0 2.3 collective-permute-start.5
  638.3 96.7 %collective-permute-done.4 = bf16[768,1536]{1,0:T(8,128)(2,1)} collective-permute-done((bf16[768,1536]{1,0:T(8,128)(2,1)S(1)}, bf16[768,1536]{1,0:T(8,128)(2,1)}, u32[]{:S(2)}, u32[]{:S(2)}) %collective-permute-start.4) | collective-permute-done | bytes 2359328 | tf_op jit(solution)/shard_map/ppermute | solution.py:49
  735.1 2.6 collective-permute-start.6
  737.7 10.2 %broadcast_select_fusion = bf16[4096,768]{1,0:T(8,128)(2,1)} fusion(bf16[4096,768]{1,0:T(8,128)(2,1)} %collective-permute-done, pred[]{:T(512)S(6)} %and.44, bf16[4096,1536]{1,0:T(8,128)(2,1)} %all-gather.4.cloned.1.call-done, s32[]{:T(128)S(6)} %select_n.79), kind=kLoop, calls=%fused_computation.3 | loop fusion | flops 3145728 | bytes 18874372 | tf_op jit(solution)/shard_map/jit(_where)/select_n | solution.py:27
  747.8 8.0 collective-permute-start.1
  755.9 1.9 collective-permute-start.7
  757.7 79.4 %collective-permute-done.6 = bf16[768,1536]{1,0:T(8,128)(2,1)} collective-permute-done((bf16[768,1536]{1,0:T(8,128)(2,1)}, bf16[768,1536]{1,0:T(8,128)(2,1)}, u32[]{:S(2)}, u32[]{:S(2)}) %collective-permute-start.6) | collective-permute-done | bytes 2359328 | tf_op jit(solution)/shard_map/ppermute | solution.py:49
  837.1 2.5 collective-permute-start.8
  841.2 3.3 constant_dynamic-update-slice_fusion.5
  844.5 3.2 constant_dynamic-update-slice_fusion.4
  847.7 3.3 constant_dynamic-update-slice_fusion.3
  851.0 3.4 constant_dynamic-update-slice_fusion.2
  854.4 3.3 constant_dynamic-update-slice_fusion.1
  857.7 36.8 %collective-permute-done.8 = bf16[768,1536]{1,0:T(8,128)(2,1)} collective-permute-done((bf16[768,1536]{1,0:T(8,128)(2,1)}, bf16[768,1536]{1,0:T(8,128)(2,1)}, u32[]{:S(2)}, u32[]{:S(2)}) %collective-permute-start.8) | collective-permute-done | bytes 2359328 | tf_op jit(solution)/shard_map/ppermute | solution.py:49
  894.5 3.2 constant_dynamic-update-slice_fusion
  897.7 3.0 multiply_add_fusion.1
  900.8 17.0 %fusion.7 = f32[512,1536]{1,0:T(8,128)} fusion(bf16[512,6144]{0,1:T(8,128)(2,1)} %all-gather.8.cloned.1.call-done, bf16[6144,1536]{1,0:T(8,128)(2,1)} %constant_dynamic-update-slice_fusion), kind=kOutput, calls=%fused_computation.20 | convolution fusion | flops 9663676416 | bytes 28311552 | tf_op jit(solution)/shard_map/dot_general | solution.py:11
  917.8 18.2 %multiply_add_fusion = f32[768,1536]{1,0:T(8,128)} fusion(f32[768,1536]{1,0:T(8,128)} %param.9, bf16[4096,1536]{1,0:T(8,128)(2,1)} %all-gather.4.cloned.1.call-done, bf16[4096,768]{1,0:T(8,128)(2,1)} %collective-permute-done.1, bf16[4096,768]{1,0:T(8,128)(2,1)} %broadcast_select_fusion, pred[]{:T(512)S(6)} %and.43), kind=kOutput, calls=%fused_computation.5 | convolution fusion | flops 9670361088 | bytes 34603008 | tf_op jit(solution)/shard_map/dot_general | solution.py:11
  (37 shorter events, 8.2 us)
Async XLA Ops:
  8.0 1.9 copy-start
  8.0 231.2 %reduce-scatter.3.cloned.1.call-start = ((), (), s32[]{:S(2)}) async-start(), calls=%async_computation.3 | async-start | bytes 14155776 | tf_op jit(solution)/shard_map/reduce_scatter | solution.py:57
  29.1 1.6 copy-start.2
  29.1 210.2 %all-gather.6.cloned.1.call-start = ((), (), s32[]{:S(2)}) async-start(), calls=%async_computation.6 | async-start | bytes 5242880 | tf_op jit(solution)/shard_map/all_gather | solution.py:38
  32.0 458.0 %all-gather.4.cloned.1.call-start = ((), (), s32[]{:S(2)}) async-start(), calls=%async_computation.4 | async-start | bytes 14155776 | tf_op jit(solution)/shard_map/all_gather | solution.py:60
  239.2 250.8 %copy-start.4 = (bf16[512,1536]{1,0:T(8,128)(2,1)S(1)}, bf16[512,1536]{1,0:T(8,128)(2,1)}, u32[]{:S(2)}) copy-start(bf16[512,1536]{1,0:T(8,128)(2,1)} %reduce-scatter.3.cloned.1.call-done) | copy-start | bytes 4718596
  239.3 294.6 %all-to-all-start = ((bf16[512,8,512]{0,2,1:T(8,128)(2,1)}), bf16[512,8,512]{0,2,1:T(8,128)(2,1)}, u32[]{:S(2)}, u32[]{:S(2)}) async-start(bf16[512,8,512]{0,2,1:T(8,128)(2,1)} %bitcast.24), calls=%async_computation.2 | async-start | bytes 8388608 | tf_op jit(solution)/shard_map/all_to_all | solution.py:39
  244.0 653.8 %reduce-scatter.5.cloned.1.call-start = ((), (), s32[]{:S(2)}) async-start(), calls=%async_computation.5 | async-start | bytes 5242880 | tf_op jit(solution)/shard_map/reduce_scatter | solution.py:68
  508.3 392.4 %all-gather.8.cloned.1.call-start = ((), (), s32[]{:S(2)}) async-start(), calls=%async_computation.7 | async-start | bytes 7864320 | tf_op jit(solution)/shard_map/all_gather | solution.py:62
  508.4 21.3 %slice-start = ((s8[4718592]{0:T(1024)(128)(4,1)}), s8[524288]{0:T(1024)(128)(4,1)S(1)}, s32[]{:S(2)}) async-start(s8[4718592]{0:T(1024)(128)(4,1)} %bitcast.21), calls=%async_computation.8 | async-start | bytes 1048576
  518.2 11.5 %slice-start.1 = ((s8[4718592]{0:T(1024)(128)(4,1)}), s8[4194304]{0:T(1024)(128)(4,1)S(1)}, s32[]{:S(2)}) async-start(s8[4718592]{0:T(1024)(128)(4,1)} %bitcast.21), calls=%async_computation.9 | async-start | bytes 8388608
  518.2 219.4 %collective-permute-start = (bf16[4096,768]{1,0:T(8,128)(2,1)}, bf16[4096,768]{1,0:T(8,128)(2,1)}, u32[]{:S(2)}, u32[]{:S(2)}) collective-permute-start(bf16[4096,768]{1,0:T(8,128)(2,1)} %constant_dynamic-slice_fusion), channel_id=1, source_target_pairs={{0,1},{4,5},{9,10},{13,14},{18,19},{22,23},{27,24},{31,28}} | collective-permute-start | bytes 18874376 | tf_op jit(solution)/shard_map/ppermute | solution.py:26
  532.3 101.3 %collective-permute-start.2 = (bf16[768,1536]{1,0:T(8,128)(2,1)}, bf16[768,1536]{1,0:T(8,128)(2,1)S(1)}, u32[]{:S(2)}, u32[]{:S(2)}) collective-permute-start(bf16[768,1536]{1,0:T(8,128)(2,1)} %get-tuple-element.4), channel_id=1, source_target_pairs={{0,4},{4,8},{8,12},{12,16},{16,20},{20,24},{24,28},{28,0},{1,5},{5... | collective-permute-start | bytes 7077896 | tf_op jit(solution)/shard_map/ppermute | solution.py:49
  552.1 83.9 %collective-permute-start.3 = (bf16[768,1536]{1,0:T(8,128)(2,1)}, bf16[768,1536]{1,0:T(8,128)(2,1)}, u32[]{:S(2)}, u32[]{:S(2)}) collective-permute-start(bf16[768,1536]{1,0:T(8,128)(2,1)} %get-tuple-element.4), channel_id=1, source_target_pairs={{0,28},{4,0},{8,4},{12,8},{16,12},{20,16},{24,20},{28,24},{1,29},{... | collective-permute-start | bytes 7077896 | tf_op jit(solution)/shard_map/ppermute | solution.py:52
  633.6 101.5 %collective-permute-start.4 = (bf16[768,1536]{1,0:T(8,128)(2,1)S(1)}, bf16[768,1536]{1,0:T(8,128)(2,1)}, u32[]{:S(2)}, u32[]{:S(2)}) collective-permute-start(bf16[768,1536]{1,0:T(8,128)(2,1)S(1)} %collective-permute-done.2), channel_id=1, source_target_pairs={{0,4},{4,8},{8,12},{12,16},{16,20},{20,24},{24,28},{28,0},{1,5},{5... | collective-permute-start | bytes 7077896 | tf_op jit(solution)/shard_map/ppermute | solution.py:49
  636.0 119.9 %collective-permute-start.5 = (bf16[768,1536]{1,0:T(8,128)(2,1)}, bf16[768,1536]{1,0:T(8,128)(2,1)}, u32[]{:S(2)}, u32[]{:S(2)}) collective-permute-start(bf16[768,1536]{1,0:T(8,128)(2,1)} %collective-permute-done.3), channel_id=1, source_target_pairs={{0,28},{4,0},{8,4},{12,8},{16,12},{20,16},{24,20},{28,24},{1,29},{... | collective-permute-start | bytes 7077896 | tf_op jit(solution)/shard_map/ppermute | solution.py:52
  735.1 102.1 %collective-permute-start.6 = (bf16[768,1536]{1,0:T(8,128)(2,1)}, bf16[768,1536]{1,0:T(8,128)(2,1)}, u32[]{:S(2)}, u32[]{:S(2)}) collective-permute-start(bf16[768,1536]{1,0:T(8,128)(2,1)} %collective-permute-done.4), channel_id=1, source_target_pairs={{0,4},{4,8},{8,12},{12,16},{16,20},{20,24},{24,28},{28,0},{1,5},{5... | collective-permute-start | bytes 7077896 | tf_op jit(solution)/shard_map/ppermute | solution.py:49
  747.8 170.0 %collective-permute-start.1 = (bf16[4096,768]{1,0:T(8,128)(2,1)}, bf16[4096,768]{1,0:T(8,128)(2,1)}, u32[]{:S(2)}, u32[]{:S(2)}) collective-permute-start(bf16[4096,768]{1,0:T(8,128)(2,1)} %broadcast_select_fusion), channel_id=1, source_target_pairs={{0,2},{1,3},{4,6},{5,7},{9,11},{10,8},{13,15},{14,12},{18,16},{19,... | collective-permute-start | bytes 18874376 | tf_op jit(solution)/shard_map/ppermute | solution.py:26
  755.9 98.5 %collective-permute-start.7 = (bf16[768,1536]{1,0:T(8,128)(2,1)}, bf16[768,1536]{1,0:T(8,128)(2,1)}, u32[]{:S(2)}, u32[]{:S(2)}) collective-permute-start(bf16[768,1536]{1,0:T(8,128)(2,1)} %collective-permute-done.5), channel_id=1, source_target_pairs={{0,28},{4,0},{8,4},{12,8},{16,12},{20,16},{24,20},{28,24},{1,29},{... | collective-permute-start | bytes 7077896 | tf_op jit(solution)/shard_map/ppermute | solution.py:52
  837.1 57.4 %collective-permute-start.8 = (bf16[768,1536]{1,0:T(8,128)(2,1)}, bf16[768,1536]{1,0:T(8,128)(2,1)}, u32[]{:S(2)}, u32[]{:S(2)}) collective-permute-start(bf16[768,1536]{1,0:T(8,128)(2,1)} %collective-permute-done.6), channel_id=1, source_target_pairs={{0,4},{4,8},{8,12},{12,16},{16,20},{20,24},{24,28},{28,0},{1,5},{5... | collective-permute-start | bytes 7077896 | tf_op jit(solution)/shard_map/ppermute | solution.py:49
  851.0 46.8 %copy-start.3 = (f32[512,1024]{1,0:T(8,128)S(1)}, f32[512,1024]{1,0:T(8,128)}, u32[]{:S(2)}) copy-start(f32[512,1024]{1,0:T(8,128)} %param.8) | copy-start | bytes 6291460
  917.8 18.2 %copy-start.1 = (bf16[1024,1536]{1,0:T(8,128)(2,1)S(1)}, bf16[1024,1536]{1,0:T(8,128)(2,1)}, u32[]{:S(2)}) copy-start(bf16[1024,1536]{1,0:T(8,128)(2,1)} %param.7) | copy-start | bytes 9437188
Sparse Core Ops, SparseCore 0:
  29.2 209.9 reduce-scatter.2
Sparse Core Ops, SparseCore 1:
  32.1 37.0 all-gather.5
  239.3 250.7 all-gather.3
  508.4 43.2 reduce-scatter.4
  553.4 57.5 all-gather.7
